TPU v7x, 32 devices: a whole 2x2x4 slice. The times are simulated.
32 devices in a mesh: grp: 4 (over y, core), dev: 8 (over z, x).
Axes of the slice: x: 2, y: 2, z: 4, core: 2. Of those that a mesh axis runs over, the one named last changes fastest.
Arguments:
- matrix: float32 [16384, 128], P(('grp', 'dev')), may hold values from -6 to 6
- flip_bits: int32 [16384], P(('grp', 'dev')), may hold values from 0 to 1
- sample_rows: int32 [2048], replicated, may hold values from 0 to 16383
Outputs:
- sketch: float32 [2048, 128], P(('grp', 'dev'))
- gram: float32 [128, 128], replicated
Inputs may be any that keep to these rules, and one draw needn't show every extreme that they name: `sample_rows`: rows may repeat.
All inputs are finite; a program needn't handle non-finite values.
Results may differ from a plain program's by a relative error of at most 0.000098.
Values sent between devices are 32-bit elements; how exact they have to be, the bound alone decides.
A program may use at most 64 MiB of HBM per device.

v0:
```python
import jax
import jax.numpy as jnp
from jax import lax
from jax.sharding import PartitionSpec as P


def hadamard_table(order):
    rows_idx = lax.broadcasted_iota(jnp.int32, (order, order), 0)
    cols_idx = lax.broadcasted_iota(jnp.int32, (order, order), 1)
    common = rows_idx & cols_idx
    parity = jnp.zeros((order, order), jnp.int32)
    for level in range(order.bit_length() - 1):
        parity = parity ^ common >> level & 1
    return (1 - 2 * parity).astype(jnp.float32)


def body(matrix, flip_bits, sample_rows):
    rows_dev, width = matrix.shape
    log_rows = rows_dev.bit_length() - 1
    outer = 2 ** (log_rows // 2)
    inner = rows_dev // outer
    n_inner = lax.axis_size("dev")
    n_outer = lax.axis_size("grp")
    devices = n_inner * n_outer
    my_index = lax.axis_index("grp") * n_inner + lax.axis_index("dev")
    signs = (1 - 2 * flip_bits).astype(jnp.float32)
    cube = (matrix * signs[:, None]).reshape(outer, inner, width)
    cube = jnp.einsum("ia,ajf->ijf", hadamard_table(outer), cube, precision=lax.Precision.HIGHEST)
    cube = jnp.einsum("jb,ibf->ijf", hadamard_table(inner), cube, precision=lax.Precision.HIGHEST)
    field = cube.reshape(rows_dev, width)
    pending = devices - 1
    keep_mask = devices - 1 ^ pending
    scale = 1.0 / jnp.sqrt(jnp.float32(rows_dev * devices))
    total_bits = devices.bit_length() - 1
    owner = sample_rows // rows_dev
    local_row = sample_rows % rows_dev
    picked = jnp.take(field, local_row, axis=0)
    common = owner & my_index & pending
    parity = jnp.zeros_like(common)
    for level in range(total_bits):
        parity = parity ^ common >> level & 1
    same = (owner ^ my_index) & keep_mask == 0
    weight = jnp.where(same, (1 - 2 * parity).astype(jnp.float32), jnp.float32(0.0)) * scale
    sketch = lax.psum_scatter(
        picked * weight[:, None], ("grp", "dev"), scatter_dimension=0, tiled=True
    )
    partial_gram = jnp.dot(
        sketch.T, sketch, preferred_element_type=jnp.float32, precision=lax.Precision.HIGHEST
    )
    gram = lax.psum(partial_gram, ("grp", "dev")) / sample_rows.shape[0]
    return (sketch, gram)


def solution(mesh):
    return jax.shard_map(
        body,
        mesh=mesh,
        in_specs=(P(("grp", "dev"), None), P(("grp", "dev")), P()),
        out_specs=(P(("grp", "dev"), None), P()),
        check_vma=False,
    )
```

profile of v0, /device:TPU:0, one launch (start us, length us, event | category | flops | bytes accessed | tf_op | source)
XLA Modules:
  0.0 287.5 jit_solution(661740037963289966)
XLA Ops:
  7.2 0.0 reduce-scatter.2.cloned.1.call-start
  7.2 0.0 copy-start
  7.2 0.8 broadcast_clamp_fusion
  8.0 0.0 copy-done
  8.0 0.0 copy-start.1
  8.0 0.7 copy-done.1
  8.7 1.1 broadcast_multiply_fusion
  9.8 0.5 fusion.2
  10.3 0.4 fusion
  10.8 5.5 %gather_fusion = f32[2048,128]{1,0:T(8,128)S(1)} fusion(f32[512,128]{1,0:T(8,128)S(1)} %bitcast.12, s32[2048]{0:T(1024)S(1)} %broadcast_clamp_fusion), kind=kCustom, calls=%fused_computation | custom fusion | bytes 2105344 | tf_op jit(solution)/shard_map/jit(_take)/gather | solution.py:37
  16.2 1.5 select_multiply_fusion
  17.7 0.0 reduce-scatter.2.cloned.1.call-update
  17.7 0.0 all-reduce.2.cloned.1.call-start
  17.8 139.4 %reduce-scatter.2.cloned.1.call-done = f32[64,128]{1,0:T(8,128)} async-done(((f32[2048,128]{1,0:T(8,128)}), f32[64,128]{1,0:T(8,128)}) %reduce-scatter.2.cloned.1.call-update) | async-done | bytes 32784 | tf_op jit(solution)/shard_map/reduce_scatter | solution.py:44
  157.2 1.8 fusion.65
  159.0 0.0 all-reduce.2.cloned.1.call-update
  159.0 120.2 %all-reduce.2.cloned.1.call-done = f32[128,128]{1,0:T(8,128)} async-done(((f32[128,128]{1,0:T(8,128)}), f32[128,128]{1,0:T(8,128)}) %all-reduce.2.cloned.1.call-update) | async-done | bytes 65552 | tf_op jit(solution)/shard_map/psum | solution.py:50
  279.2 1.5 broadcast_multiply_fusion.1
  (3 shorter events, 0.0 us)
Async XLA Ops:
  7.2 150.1 %reduce-scatter.2.cloned.1.call-start = ((), (), s32[]{:S(2)}) async-start(), calls=%async_computation.1 | async-start | bytes 1081344 | tf_op jit(solution)/shard_map/reduce_scatter | solution.py:44
  7.2 0.8 copy-start
  8.0 0.7 copy-start.1
  17.7 261.5 %all-reduce.2.cloned.1.call-start = ((), (), s32[]{:S(2)}) async-start(), calls=%async_computation.2 | async-start | bytes 131072 | tf_op jit(solution)/shard_map/psum | solution.py:50
Sparse Core Ops, SparseCore 0:
  17.9 139.3 reduce-scatter.1
  163.4 115.8 all-reduce.1
where the time goes:
time: 289 us; the launch traced here: 288 us
  waiting for transfers between devices  260 us (90%)
  between operations  14.1 us (5%)
  local copies, waits for them, and re-layouts  6.13 us (2%)
  other arithmetic  4.86 us (2%)
    reduce_scatter x1, waiting for transfers between devices, body(): lax.psum_scatter(picked * weight[:, None], ('grp', 'dev'), scatter_dimens...  139 us
    psum x1, waiting for transfers between devices, body(): gram = lax.psum(partial_gram, ('grp', 'dev')) / sample_rows.shape[0]  120 us
  transfers between devices with their start and end apart: 2, of which 2 were waited for; matrix products, arithmetic and copies ran while one was open for 0% of the time, Pallas kernels for 0%

commit v1 on v0

v1 whole, which is shorter than its diff:
```python
import functools
import math

import jax
import jax.numpy as jnp
from jax import lax
from jax.experimental import pallas as pl
from jax.experimental.pallas import tpu as pltpu
from jax.sharding import PartitionSpec as P

MESH = pl.DeviceIdType.MESH
LANES = 128


def loop(count, fn):
    if count <= 8:
        for step in range(count):
            fn(step)
    else:
        lax.fori_loop(0, count, lambda step, carry: (fn(step), carry)[1], 0)


def parity(bits, width):
    shift = 1
    while shift * 2 < width:
        shift *= 2
    while shift:
        bits = bits ^ (bits >> shift)
        shift //= 2
    return bits & 1


def sign_of(bits, width):
    return (1 - 2 * parity(bits, width)).astype(jnp.float32)


def split3(value):
    high = value.astype(jnp.bfloat16)
    rest = value - high.astype(jnp.float32)
    mid = rest.astype(jnp.bfloat16)
    low = (rest - mid.astype(jnp.float32)).astype(jnp.bfloat16)
    return high, mid, low


def kernel(
    n_grp, n_dev, rows, own,
    x_ref, flip_ref, sample_ref, sketch_ref, gram_ref,
    slabs, flips, cols, index, base, part, blocks, gpart, gslots, gfull, reduced,
    load_sem, pair_send, pair_recv, twin_send, twin_recv, fwd_send, fwd_recv,
    flip_send, flip_recv, rs_send, rs_recv, g_send, g_recv, b_send, b_recv,
):
    f32 = jnp.float32
    devices = n_grp * n_dev
    n_y, n_z = n_grp // 2, n_dev // 2
    groups = n_y * n_z
    chips = devices // 2
    width = x_ref.shape[1]
    pieces = twin_send.shape[0]
    piece = rows // pieces
    samples = sample_ref.shape[0] * LANES
    row_bits = rows.bit_length() - 1
    all_bits = (rows * devices).bit_length() - 1
    me_g, me_d = lax.axis_index("grp"), lax.axis_index("dev")
    core, y = lax.rem(me_g, 2), lax.div(me_g, 2)
    x, z = lax.rem(me_d, 2), lax.div(me_d, 2)
    pair_g = me_g + 1 - 2 * core
    twin_d = me_d + 1 - 2 * x
    mine = y * n_z + z

    def remote(src, dst, send, recv, grp, dev):
        return pltpu.make_async_remote_copy(
            src_ref=src, dst_ref=dst, send_sem=send, recv_sem=recv,
            device_id=(grp, dev), device_id_type=MESH,
        )

    barrier = pltpu.get_barrier_semaphore()

    def greet(i, j):
        pl.semaphore_signal(
            barrier, inc=1,
            device_id=(lax.rem(me_g + i, n_grp), lax.rem(me_d + j, n_dev)),
            device_id_type=MESH,
        )

    for i in range(n_grp):
        loop(n_dev - (i == 0), lambda j: greet(i, j + (i == 0)))

    load = pltpu.make_async_copy(x_ref, slabs.at[0], load_sem)
    load.start()
    pl.semaphore_wait(barrier, devices - 1)

    twin = []
    for c in range(pieces):
        at = pl.ds(c * piece, piece)
        copy = remote(x_ref.at[at], slabs.at[2, at], twin_send.at[c], twin_recv.at[c], me_g, twin_d)
        copy.start()
        twin.append(copy)
    pair = remote(x_ref, slabs.at[1], pair_send, pair_recv, pair_g, me_d)
    pair.start()
    flip_copies = [
        remote(flip_ref, flips.at[0], flip_send.at[0], flip_recv.at[0], pair_g, me_d),
        remote(flip_ref, flips.at[1], flip_send.at[1], flip_recv.at[1], me_g, twin_d),
        remote(flip_ref, flips.at[2], flip_send.at[2], flip_recv.at[2], pair_g, twin_d),
    ]
    for copy in flip_copies:
        copy.start()

    span = n_dev * own // LANES
    for i in range(n_y):
        for r in range(span):
            line = sample_ref[pl.ds((i * 2 + core) * span + r, 1), :]
            cols[pl.ds((i * span + r) * LANES, LANES), :] = jnp.transpose(
                jnp.broadcast_to(line, (LANES, LANES))
            )
    for i in range(n_y):
        for j in range(n_z):
            index[pl.ds((i * n_z + j) * own, own), :] = cols[
                pl.ds((i * n_dev + j * 2 + x) * own, own), :
            ]
    picks = groups * own
    wanted = index[...]
    for k in range(rows // LANES):
        lane = lax.broadcasted_iota(jnp.int32, (picks, LANES), 1) + k * LANES
        base[:, k * LANES:(k + 1) * LANES] = sign_of(wanted & lane, row_bits).astype(jnp.bfloat16)

    def term(slot, flip_bits, grp, dev):
        signs = base[...]
        toggles = (1 - 2 * flip_bits).astype(f32).astype(jnp.bfloat16)
        signs = jnp.concatenate(
            [
                signs[:, k * LANES:(k + 1) * LANES] * toggles[k:k + 1, :]
                for k in range(rows // LANES)
            ],
            axis=1,
        )
        total = None
        for piece_of in split3(slabs[slot]):
            product = jnp.dot(signs, piece_of, preferred_element_type=f32)
            total = product if total is None else total + product
        place = (grp * n_dev + dev) * rows
        return total * sign_of(wanted & place, all_bits)

    load.wait()
    total = term(0, flip_ref[...], me_g, me_d)
    flip_copies[0].wait_recv()
    pair.wait_recv()
    total = total + term(1, flips[0], pair_g, me_d)
    forward = []
    for c in range(pieces):
        at = pl.ds(c * piece, piece)
        twin[c].wait_recv()
        copy = remote(slabs.at[2, at], slabs.at[3, at], fwd_send.at[c], fwd_recv.at[c], pair_g, me_d)
        copy.start()
        forward.append(copy)
    flip_copies[1].wait_recv()
    total = total + term(2, flips[1], me_g, twin_d)
    for copy in forward:
        copy.wait_recv()
    flip_copies[2].wait_recv()
    total = total + term(3, flips[2], pair_g, twin_d)
    part[...] = total.reshape(groups, own, width)

    def give(i, j):
        to_y, to_z = lax.rem(y + i, n_y), lax.rem(z + j, n_z)
        remote(
            part.at[to_y * n_z + to_z], blocks.at[mine], rs_send, rs_recv,
            to_y * 2 + core, to_z * 2 + x,
        ).start()

    for i in range(n_y - 1, -1, -1):
        loop(n_z - (i == 0), lambda j: give(i, j + (i == 0)))
    blocks[mine] = part[mine]
    others = blocks.at[pl.ds(0, groups - 1)]
    pltpu.make_async_copy(others, others, rs_recv).wait()
    sketch = blocks[0]
    for i in range(1, groups):
        sketch = sketch + blocks[i]
    sketch = sketch * (1.0 / math.sqrt(rows * devices))
    sketch_ref[...] = sketch

    chunks = gfull.shape[0]
    stride = chips // chunks
    chunk = width // chunks
    my_chip = y * n_dev + me_d
    linear = me_g * n_dev + me_d
    reducer = (core == 0) & (lax.rem(my_chip, stride) == 0)
    my_chunk = lax.div(my_chip, stride)
    gram = lax.dot_general(
        sketch, sketch, (((0,), (0,)), ((), ())),
        precision=lax.Precision.HIGHEST, preferred_element_type=f32,
    )
    gpart[...] = gram.reshape(chunks, chunk, width)
    for k in range(chunks):
        to_g, to_d = (k * stride) // n_dev * 2, (k * stride) % n_dev

        @pl.when((me_g != to_g) | (me_d != to_d))
        def _():
            remote(gpart.at[k], gslots.at[linear], g_send, g_recv, to_g, to_d).start()

    @pl.when(reducer)
    def _():
        gslots[linear] = gpart[my_chunk]
        rest = gslots.at[pl.ds(0, devices - 1)]
        pltpu.make_async_copy(rest, rest, g_recv).wait()
        result = jnp.sum(gslots[...], axis=0) * (1.0 / samples)
        reduced[...] = result
        gfull[my_chunk] = result

        def tell(i, j):
            remote(
                reduced, gfull.at[my_chunk], b_send, b_recv,
                lax.rem(me_g + i, n_grp), lax.rem(me_d + j, n_dev),
            ).start()

        for i in range(n_grp - 1, -1, -1):
            loop(n_dev - (i == 0), lambda j: tell(i, j + (i == 0)))
        most = gfull.at[pl.ds(0, chunks - 1)]
        pltpu.make_async_copy(most, most, b_recv).wait()
        pltpu.make_async_copy(rest, rest, b_send).wait()
        pltpu.make_async_copy(most, most, g_send).wait()

    @pl.when(jnp.logical_not(reducer))
    def _():
        pltpu.make_async_copy(gfull, gfull, b_recv).wait()
        pltpu.make_async_copy(gfull, gfull, g_send).wait()

    gram_ref[...] = gfull[...].reshape(width, width)
    for copy in twin + forward + flip_copies + [pair]:
        copy.wait_send()
    pltpu.make_async_copy(others, others, rs_send).wait()


def body(matrix, flip_bits, sample_rows):
    rows, width = matrix.shape
    n_grp, n_dev = lax.axis_size("grp"), lax.axis_size("dev")
    devices = n_grp * n_dev
    samples = sample_rows.shape[0]
    own = samples // devices
    groups = devices // 4
    chunks = min(width // 8, devices // 2)
    chunk = width // chunks
    pieces = 4
    f32, i32 = jnp.float32, jnp.int32
    dma = pltpu.SemaphoreType.DMA
    vmem = pl.BlockSpec(memory_space=pltpu.VMEM)
    return pl.pallas_call(
        functools.partial(kernel, n_grp, n_dev, rows, own),
        out_shape=(
            jax.ShapeDtypeStruct((own, width), f32),
            jax.ShapeDtypeStruct((width, width), f32),
        ),
        in_specs=[pl.BlockSpec(memory_space=pl.ANY), vmem, vmem],
        out_specs=(vmem, vmem),
        scratch_shapes=[
            pltpu.VMEM((4, rows, width), f32),
            pltpu.VMEM((3, rows // LANES, LANES), i32),
            pltpu.VMEM((samples // 2, LANES), i32),
            pltpu.VMEM((groups * own, LANES), i32),
            pltpu.VMEM((groups * own, rows), jnp.bfloat16),
            pltpu.VMEM((groups, own, width), f32),
            pltpu.VMEM((groups, own, width), f32),
            pltpu.VMEM((chunks, chunk, width), f32),
            pltpu.VMEM((devices, chunk, width), f32),
            pltpu.VMEM((chunks, chunk, width), f32),
            pltpu.VMEM((chunk, width), f32),
            dma, dma, dma, dma((pieces,)), dma((pieces,)), dma((pieces,)), dma((pieces,)),
            dma((3,)), dma((3,)), dma, dma, dma, dma, dma, dma,
        ],
        compiler_params=pltpu.CompilerParams(collective_id=0, has_side_effects=True),
    )(
        matrix,
        flip_bits.reshape(rows // LANES, LANES),
        sample_rows.reshape(samples // LANES, LANES),
    )


def solution(mesh):
    return jax.shard_map(
        body,
        mesh=mesh,
        in_specs=(P(("grp", "dev"), None), P(("grp", "dev")), P()),
        out_specs=(P(("grp", "dev"), None), P()),
        check_vma=False,
    )
```

time: 289 us -> 37.6 us (0.13)
  waiting for transfers between devices: 260 us -> 0 us
  Pallas kernels: 0 us -> 34.7 us
  between operations: 14.1 us -> 0.65 us
  other arithmetic: 4.86 us -> 0 us
  local copies, waits for them, and re-layouts: 6.13 us -> 2.04 us
    reduce_scatter x1 -> x0, waiting for transfers between devices: 139 us -> none  [body(): lax.psum_scatter(picked * weight[:, None], ('grp', 'dev'), scatter_dimens...]
    psum x1 -> x0, waiting for transfers between devices: 120 us -> none  [body(): gram = lax.psum(partial_gram, ('grp', 'dev')) / sample_rows.shape[0]]
    pallas_call x0 -> x1, Pallas kernels: none -> 34.7 us  [body(): pl.pallas_call(functools.partial(kernel, n_grp, n_dev, rows, own), out_sh...]
    gather x1 -> x0, local copies, waits for them, and re-layouts: 5.47 us -> none  [body(): picked = jnp.take(field, local_row, axis=0)]
  transfers between devices with their start and end apart: 2 -> 0, of which waited for: 2 -> 0; matrix products, arithmetic and copies ran while one was open for 0% -> 0% of each run, Pallas kernels for 0% -> 0%
where the time goes in v1:
time: 37.6 us; the launch traced here: 37.3 us
  Pallas kernels  34.7 us (92%)
  local copies, waits for them, and re-layouts  2.04 us (5%)
  between operations  0.65 us (2%)
    pallas_call x1, Pallas kernels, body(): pl.pallas_call(functools.partial(kernel, n_grp, n_dev, rows, own), out_sh...  34.7 us
    unnamed x4, local copies, waits for them, and re-layouts  2.04 us

profile of v1, /device:TPU:0, one launch (start us, length us, event | category | flops | bytes accessed | tf_op | source)
XLA Modules:
  0.0 37.3 jit_solution(14127904738323858466)
XLA Ops:
  0.6 34.7 %shard_map.50 = (f32[64,128]{1,0:T(8,128)}, f32[128,128]{1,0:T(8,128)}) custom-call(f32[512,128]{1,0:T(8,128)} %x_ref.1, s32[4,128]{1,0:T(4,128)} %bitcast.3, s32[16,128]{1,0:T(8,128)} %bitcast.2), custom_call_target="tpu_custom_call" | custom-call | tf_op jit(solution)/shard_map/pallas_call | solution.py:246
  35.3 0.0 copy-start
  35.3 1.4 %copy.7 = f32[64,128]{1,0:T(8,128)} copy(f32[64,128]{1,0:T(8,128)} %get-tuple-element.4) | data formatting | bytes 65536
  36.7 0.0 copy-done
  36.7 0.6 %copy.8 = f32[128,128]{1,0:T(8,128)} copy(f32[128,128]{1,0:T(8,128)S(1)} %copy-done) | data formatting | bytes 131072
Async XLA Ops:
  35.3 1.4 %copy-start = (f32[128,128]{1,0:T(8,128)S(1)}, f32[128,128]{1,0:T(8,128)}, u32[]{:S(2)}) copy-start(f32[128,128]{1,0:T(8,128)} %get-tuple-element.5) | copy-start | bytes 196612

commit v2 on v1

--- a/solution.py
+++ b/solution.py
@@ -44,20 +44,20 @@
 
 def kernel(
     n_grp, n_dev, rows, own,
-    x_ref, flip_ref, sample_ref, sketch_ref, gram_ref,
-    slabs, flips, cols, index, base, part, blocks, gpart, gslots, gfull, reduced,
+    x_ref, flip_hbm, sample_hbm, sketch_ref, gram_ref,
+    flip_ref, sample_ref, slabs, flips, cols, index, base, part, blocks, gpart, gslots, gfull, reduced,
     load_sem, pair_send, pair_recv, twin_send, twin_recv, fwd_send, fwd_recv,
     flip_send, flip_recv, rs_send, rs_recv, g_send, g_recv, b_send, b_recv,
+    ready,
 ):
     f32 = jnp.float32
     devices = n_grp * n_dev
     n_y, n_z = n_grp // 2, n_dev // 2
     groups = n_y * n_z
-    chips = devices // 2
     width = x_ref.shape[1]
     pieces = twin_send.shape[0]
     piece = rows // pieces
-    samples = sample_ref.shape[0] * LANES
+    samples = sample_hbm.shape[0] * LANES
     row_bits = rows.bit_length() - 1
     all_bits = (rows * devices).bit_length() - 1
     me_g, me_d = lax.axis_index("grp"), lax.axis_index("dev")
@@ -75,19 +75,65 @@
 
     barrier = pltpu.get_barrier_semaphore()
 
-    def greet(i, j):
-        pl.semaphore_signal(
-            barrier, inc=1,
-            device_id=(lax.rem(me_g + i, n_grp), lax.rem(me_d + j, n_dev)),
-            device_id_type=MESH,
-        )
-
-    for i in range(n_grp):
-        loop(n_dev - (i == 0), lambda j: greet(i, j + (i == 0)))
-
-    load = pltpu.make_async_copy(x_ref, slabs.at[0], load_sem)
-    load.start()
-    pl.semaphore_wait(barrier, devices - 1)
+    def signal(sem, grp, dev):
+        pl.semaphore_signal(sem, inc=1, device_id=(grp, dev), device_id_type=MESH)
+
+    def along_y(step):
+        return me_g + 2 * step, me_d
+
+    def along_z(step):
+        return me_g, me_d + 2 * step
+
+    def tell_line(sem, at, size, reach, along):
+        for step in range(1, min(reach, size - 1) + 1):
+            @pl.when(at >= step)
+            def _():
+                signal(sem, *along(-step))
+
+            @pl.when(at + step < size)
+            def _():
+                signal(sem, *along(step))
+
+    def line_count(at, size, reach):
+        return jnp.minimum(at, reach) + jnp.minimum(size - 1 - at, reach)
+
+    signal(barrier, pair_g, me_d)
+    signal(barrier, me_g, twin_d)
+    tell_line(barrier, y, n_y, 1, along_y)
+    tell_line(barrier, z, n_z, 1, along_z)
+
+    loads = [
+        pltpu.make_async_copy(sample_hbm, sample_ref, load_sem.at[0]),
+        pltpu.make_async_copy(flip_hbm, flip_ref, load_sem.at[1]),
+        pltpu.make_async_copy(x_ref, slabs.at[0], load_sem.at[2]),
+    ]
+    for copy in loads:
+        copy.start()
+    pl.semaphore_wait(barrier, 2 + line_count(y, n_y, 1) + line_count(z, n_z, 1))
+
+    rounds = []
+    for at, size, along in ((z, n_z, along_z), (y, n_y, along_y)):
+        reach = 1
+        while reach < size - 1:
+            rounds.append((at, size, reach, along))
+            reach *= 2
+    rounds.append((y, n_y, n_y - 1, along_y))
+
+    def open_round(k):
+        if k < len(rounds):
+            at, size, reach, along = rounds[k]
+            tell_line(ready.at[k], at, size, reach, along)
+        elif k == len(rounds):
+            signal(ready.at[k], me_g, twin_d)
+        else:
+            signal(ready.at[k], pair_g, me_d)
+
+    def close_round(k):
+        if k < len(rounds):
+            at, size, reach, along = rounds[k]
+            pl.semaphore_wait(ready.at[k], line_count(at, size, reach))
+        else:
+            pl.semaphore_wait(ready.at[k], 1)
 
     twin = []
     for c in range(pieces):
@@ -100,9 +146,12 @@
     flip_copies = [
         remote(flip_ref, flips.at[0], flip_send.at[0], flip_recv.at[0], pair_g, me_d),
         remote(flip_ref, flips.at[1], flip_send.at[1], flip_recv.at[1], me_g, twin_d),
-        remote(flip_ref, flips.at[2], flip_send.at[2], flip_recv.at[2], pair_g, twin_d),
+        remote(flips.at[1], flips.at[2], flip_send.at[2], flip_recv.at[2], pair_g, me_d),
     ]
-    for copy in flip_copies:
+    open_round(0)
+    for copy in loads:
+        copy.wait()
+    for copy in flip_copies[:2]:
         copy.start()
 
     span = n_dev * own // LANES
@@ -117,6 +166,8 @@
             index[pl.ds((i * n_z + j) * own, own), :] = cols[
                 pl.ds((i * n_dev + j * 2 + x) * own, own), :
             ]
+    close_round(0)
+    open_round(1)
     picks = groups * own
     wanted = index[...]
     for k in range(rows // LANES):
@@ -140,8 +191,12 @@
         place = (grp * n_dev + dev) * rows
         return total * sign_of(wanted & place, all_bits)
 
-    load.wait()
+    for k in range(1, len(rounds) - 1):
+        close_round(k)
+        open_round(k + 1)
     total = term(0, flip_ref[...], me_g, me_d)
+    close_round(len(rounds) - 1)
+    open_round(len(rounds))
     flip_copies[0].wait_recv()
     pair.wait_recv()
     total = total + term(1, flips[0], pair_g, me_d)
@@ -153,6 +208,9 @@
         copy.start()
         forward.append(copy)
     flip_copies[1].wait_recv()
+    flip_copies[2].start()
+    close_round(len(rounds))
+    open_round(len(rounds) + 1)
     total = total + term(2, flips[1], me_g, twin_d)
     for copy in forward:
         copy.wait_recv()
@@ -178,20 +236,21 @@
     sketch = sketch * (1.0 / math.sqrt(rows * devices))
     sketch_ref[...] = sketch
 
+    close_round(len(rounds) + 1)
     chunks = gfull.shape[0]
-    stride = chips // chunks
+    across = min(chunks, n_dev // 2)
+    first = (n_dev - across) // 2
     chunk = width // chunks
-    my_chip = y * n_dev + me_d
     linear = me_g * n_dev + me_d
-    reducer = (core == 0) & (lax.rem(my_chip, stride) == 0)
-    my_chunk = lax.div(my_chip, stride)
+    reducer = (me_g < chunks // across) & (me_d >= first) & (me_d < first + across)
+    my_chunk = me_g * across + me_d - first
     gram = lax.dot_general(
         sketch, sketch, (((0,), (0,)), ((), ())),
         precision=lax.Precision.HIGHEST, preferred_element_type=f32,
     )
     gpart[...] = gram.reshape(chunks, chunk, width)
     for k in range(chunks):
-        to_g, to_d = (k * stride) // n_dev * 2, (k * stride) % n_dev
+        to_g, to_d = k // across, first + k % across
 
         @pl.when((me_g != to_g) | (me_d != to_d))
         def _():
@@ -246,12 +305,14 @@
     return pl.pallas_call(
         functools.partial(kernel, n_grp, n_dev, rows, own),
         out_shape=(
-            jax.ShapeDtypeStruct((own, width), f32),
-            jax.ShapeDtypeStruct((width, width), f32),
+            pltpu.VMEM((own, width), f32),
+            pltpu.VMEM((width, width), f32),
         ),
-        in_specs=[pl.BlockSpec(memory_space=pl.ANY), vmem, vmem],
+        in_specs=[pl.BlockSpec(memory_space=pl.ANY)] * 3,
         out_specs=(vmem, vmem),
         scratch_shapes=[
+            pltpu.VMEM((rows // LANES, LANES), i32),
+            pltpu.VMEM((samples // LANES, LANES), i32),
             pltpu.VMEM((4, rows, width), f32),
             pltpu.VMEM((3, rows // LANES, LANES), i32),
             pltpu.VMEM((samples // 2, LANES), i32),
@@ -263,8 +324,9 @@
             pltpu.VMEM((devices, chunk, width), f32),
             pltpu.VMEM((chunks, chunk, width), f32),
             pltpu.VMEM((chunk, width), f32),
-            dma, dma, dma, dma((pieces,)), dma((pieces,)), dma((pieces,)), dma((pieces,)),
+            dma((3,)), dma, dma, dma((pieces,)), dma((pieces,)), dma((pieces,)), dma((pieces,)),
             dma((3,)), dma((3,)), dma, dma, dma, dma, dma, dma,
+            pltpu.SemaphoreType.REGULAR((16,)),
         ],
         compiler_params=pltpu.CompilerParams(collective_id=0, has_side_effects=True),
     )(

time: 37.6 us -> 33.4 us (0.89)
  Pallas kernels: 34.7 us -> 31.4 us
  local copies, waits for them, and re-layouts: 2.04 us -> 1.25 us
    pallas_call x1, Pallas kernels: 34.7 us -> 31.4 us  [body(): pl.pallas_call(functools.partial(kernel, n_grp, n_dev, rows, own), out_sh...]
    unnamed x4 -> x2, local copies, waits for them, and re-layouts: 2.04 us -> 1.25 us
where the time goes in v2:
time: 33.4 us; the launch traced here: 33.2 us
  Pallas kernels  31.4 us (94%)
  local copies, waits for them, and re-layouts  1.25 us (4%)
  between operations  0.64 us (2%)
    pallas_call x1, Pallas kernels, body(): pl.pallas_call(functools.partial(kernel, n_grp, n_dev, rows, own), out_sh...  31.4 us
    unnamed x2, local copies, waits for them, and re-layouts  1.25 us

profile of v2, /device:TPU:0, one launch (start us, length us, event | category | flops | bytes accessed | tf_op | source)
XLA Modules:
  0.0 33.2 jit_solution(9534240048817463765)
XLA Ops:
  0.6 31.4 %shard_map.50 = (f32[64,128]{1,0:T(8,128)S(1)}, f32[128,128]{1,0:T(8,128)S(1)}) custom-call(f32[512,128]{1,0:T(8,128)} %x_ref.1, s32[4,128]{1,0:T(4,128)} %bitcast.3, s32[16,128]{1,0:T(8,128)} %bitcast.2), custom_call_target="tpu_custom_call" | custom-call | tf_op jit(solution)/shard_map/pallas_call | solution.py:305
  32.0 0.6 %copy.7 = f32[64,128]{1,0:T(8,128)} copy(f32[64,128]{1,0:T(8,128)S(1)} %get-tuple-element.2) | data formatting | bytes 65536
  32.6 0.6 %copy.8 = f32[128,128]{1,0:T(8,128)} copy(f32[128,128]{1,0:T(8,128)S(1)} %get-tuple-element.3) | data formatting | bytes 131072

commit v3 on v2

--- a/solution.py
+++ b/solution.py
@@ -45,7 +45,7 @@
 def kernel(
     n_grp, n_dev, rows, own,
     x_ref, flip_hbm, sample_hbm, sketch_ref, gram_ref,
-    flip_ref, sample_ref, slabs, flips, cols, index, base, part, blocks, gpart, gslots, gfull, reduced,
+    flip_ref, sample_ref, x_full, slabs, flips, cols, index, base, part, blocks, gpart, gslots, gfull, reduced,
     load_sem, pair_send, pair_recv, twin_send, twin_recv, fwd_send, fwd_recv,
     flip_send, flip_recv, rs_send, rs_recv, g_send, g_recv, b_send, b_recv,
     ready,
@@ -105,7 +105,7 @@
     loads = [
         pltpu.make_async_copy(sample_hbm, sample_ref, load_sem.at[0]),
         pltpu.make_async_copy(flip_hbm, flip_ref, load_sem.at[1]),
-        pltpu.make_async_copy(x_ref, slabs.at[0], load_sem.at[2]),
+        pltpu.make_async_copy(x_ref, x_full, load_sem.at[2]),
     ]
     for copy in loads:
         copy.start()
@@ -135,22 +135,40 @@
         else:
             pl.semaphore_wait(ready.at[k], 1)
 
-    twin = []
-    for c in range(pieces):
-        at = pl.ds(c * piece, piece)
-        copy = remote(x_ref.at[at], slabs.at[2, at], twin_send.at[c], twin_recv.at[c], me_g, twin_d)
+    half = width // 2
+    left = lax.broadcasted_iota(jnp.int32, (1, width), 1) < half
+
+    def swap(value):
+        return pltpu.roll(value, half, value.ndim - 1)
+
+    for copy in loads:
+        copy.wait()
+    top, bottom = x_full[pl.ds(0, rows // 2), :], x_full[pl.ds(rows // 2, rows // 2), :]
+    slabs[0, 0] = jnp.where(left, top, swap(bottom))
+    slabs[1, 0] = jnp.where(left, swap(top), bottom)
+    twin, pair = [], []
+    for h in range(2):
+        for c in range(pieces // 2):
+            at = pl.ds(c * piece, piece)
+            k = h * (pieces // 2) + c
+            copy = remote(
+                slabs.at[h, 0, at], slabs.at[h, 2, at],
+                twin_send.at[k], twin_recv.at[k], me_g, twin_d,
+            )
+            copy.start()
+            twin.append(copy)
+    for h in range(2):
+        copy = remote(
+            slabs.at[h, 0], slabs.at[h, 1], pair_send.at[h], pair_recv.at[h], pair_g, me_d
+        )
         copy.start()
-        twin.append(copy)
-    pair = remote(x_ref, slabs.at[1], pair_send, pair_recv, pair_g, me_d)
-    pair.start()
+        pair.append(copy)
     flip_copies = [
         remote(flip_ref, flips.at[0], flip_send.at[0], flip_recv.at[0], pair_g, me_d),
         remote(flip_ref, flips.at[1], flip_send.at[1], flip_recv.at[1], me_g, twin_d),
         remote(flips.at[1], flips.at[2], flip_send.at[2], flip_recv.at[2], pair_g, me_d),
     ]
     open_round(0)
-    for copy in loads:
-        copy.wait()
     for copy in flip_copies[:2]:
         copy.start()
 
@@ -174,7 +192,7 @@
         lane = lax.broadcasted_iota(jnp.int32, (picks, LANES), 1) + k * LANES
         base[:, k * LANES:(k + 1) * LANES] = sign_of(wanted & lane, row_bits).astype(jnp.bfloat16)
 
-    def term(slot, flip_bits, grp, dev):
+    def term(h, slot, flip_bits, grp, dev):
         signs = base[...]
         toggles = (1 - 2 * flip_bits).astype(f32).astype(jnp.bfloat16)
         signs = jnp.concatenate(
@@ -184,55 +202,83 @@
             ],
             axis=1,
         )
-        total = None
-        for piece_of in split3(slabs[slot]):
-            product = jnp.dot(signs, piece_of, preferred_element_type=f32)
-            total = product if total is None else total + product
+        packed = slabs[h, slot]
+        high, mid, low = split3(packed)
+        high_s, mid_s, low_s = split3(swap(packed))
+        right = jnp.concatenate(
+            [
+                jnp.concatenate([jnp.where(left, high, mid_s), low], axis=1),
+                jnp.concatenate([jnp.where(left, high_s, mid), low_s], axis=1),
+            ],
+            axis=0,
+        )
+        product = jnp.dot(signs, right, preferred_element_type=f32)
+        first, last = product[:, :width], product[:, width:]
         place = (grp * n_dev + dev) * rows
-        return total * sign_of(wanted & place, all_bits)
+        return (first + swap(first) + last) * sign_of(wanted & place, all_bits)
+
+    def give(h, i, j):
+        to_y, to_z = lax.rem(y + i, n_y), lax.rem(z + j, n_z)
+        remote(
+            part.at[h, to_y * n_z + to_z], blocks.at[h, mine], rs_send.at[h], rs_recv.at[h],
+            to_y * 2 + core, to_z * 2 + x,
+        ).start()
 
     for k in range(1, len(rounds) - 1):
         close_round(k)
         open_round(k + 1)
-    total = term(0, flip_ref[...], me_g, me_d)
+    totals = [term(h, 0, flip_ref[...], me_g, me_d) for h in range(2)]
     close_round(len(rounds) - 1)
     open_round(len(rounds))
     flip_copies[0].wait_recv()
-    pair.wait_recv()
-    total = total + term(1, flips[0], pair_g, me_d)
-    forward = []
-    for c in range(pieces):
-        at = pl.ds(c * piece, piece)
-        twin[c].wait_recv()
-        copy = remote(slabs.at[2, at], slabs.at[3, at], fwd_send.at[c], fwd_recv.at[c], pair_g, me_d)
-        copy.start()
-        forward.append(copy)
+    for h in range(2):
+        pair[h].wait_recv()
+        totals[h] = totals[h] + term(h, 1, flips[0], pair_g, me_d)
     flip_copies[1].wait_recv()
     flip_copies[2].start()
-    close_round(len(rounds))
-    open_round(len(rounds) + 1)
-    total = total + term(2, flips[1], me_g, twin_d)
-    for copy in forward:
-        copy.wait_recv()
-    flip_copies[2].wait_recv()
-    total = total + term(3, flips[2], pair_g, twin_d)
-    part[...] = total.reshape(groups, own, width)
-
-    def give(i, j):
-        to_y, to_z = lax.rem(y + i, n_y), lax.rem(z + j, n_z)
-        remote(
-            part.at[to_y * n_z + to_z], blocks.at[mine], rs_send, rs_recv,
-            to_y * 2 + core, to_z * 2 + x,
-        ).start()
-
-    for i in range(n_y - 1, -1, -1):
-        loop(n_z - (i == 0), lambda j: give(i, j + (i == 0)))
-    blocks[mine] = part[mine]
-    others = blocks.at[pl.ds(0, groups - 1)]
-    pltpu.make_async_copy(others, others, rs_recv).wait()
-    sketch = blocks[0]
-    for i in range(1, groups):
-        sketch = sketch + blocks[i]
+    forward = []
+    for h in range(2):
+        for c in range(pieces // 2):
+            at = pl.ds(c * piece, piece)
+            k = h * (pieces // 2) + c
+            twin[k].wait_recv()
+            copy = remote(
+                slabs.at[h, 2, at], slabs.at[h, 3, at],
+                fwd_send.at[k], fwd_recv.at[k], pair_g, me_d,
+            )
+            copy.start()
+            forward.append(copy)
+        total = totals[h] + term(h, 2, flips[1], me_g, twin_d)
+        if h == 0:
+            flip_copies[2].wait_recv()
+        for copy in forward[h * (pieces // 2):]:
+            copy.wait_recv()
+        total = total + term(h, 3, flips[2], pair_g, twin_d)
+        total = total.reshape(groups, own, width)
+        part[h] = jnp.where(
+            left.reshape(1, 1, width), total[:, :own // 2], swap(total[:, own // 2:])
+        )
+        if h == 0:
+            close_round(len(rounds))
+            open_round(len(rounds) + 1)
+        for i in range(n_y - 1, -1, -1):
+            loop(n_z - (i == 0), lambda j: give(h, i, j + (i == 0)))
+        blocks[h, mine] = part[h, mine]
+    sums = []
+    for h in range(2):
+        others = blocks.at[h, pl.ds(0, groups - 1)]
+        pltpu.make_async_copy(others, others, rs_recv.at[h]).wait()
+        summed = blocks[h, 0]
+        for i in range(1, groups):
+            summed = summed + blocks[h, i]
+        sums.append(summed)
+    sketch = jnp.concatenate(
+        [
+            jnp.where(left, sums[0], swap(sums[1])),
+            jnp.where(left, swap(sums[0]), sums[1]),
+        ],
+        axis=0,
+    )
     sketch = sketch * (1.0 / math.sqrt(rows * devices))
     sketch_ref[...] = sketch
 
@@ -249,12 +295,14 @@
         precision=lax.Precision.HIGHEST, preferred_element_type=f32,
     )
     gpart[...] = gram.reshape(chunks, chunk, width)
+    turn = lax.rem(linear, chunks)
     for k in range(chunks):
-        to_g, to_d = k // across, first + k % across
+        to = lax.rem(k + turn, chunks)
+        to_g, to_d = lax.div(to, across), first + lax.rem(to, across)
 
         @pl.when((me_g != to_g) | (me_d != to_d))
         def _():
-            remote(gpart.at[k], gslots.at[linear], g_send, g_recv, to_g, to_d).start()
+            remote(gpart.at[to], gslots.at[linear], g_send, g_recv, to_g, to_d).start()
 
     @pl.when(reducer)
     def _():
@@ -284,9 +332,11 @@
         pltpu.make_async_copy(gfull, gfull, g_send).wait()
 
     gram_ref[...] = gfull[...].reshape(width, width)
-    for copy in twin + forward + flip_copies + [pair]:
+    for copy in twin + forward + flip_copies + pair:
         copy.wait_send()
-    pltpu.make_async_copy(others, others, rs_send).wait()
+    for h in range(2):
+        others = blocks.at[h, pl.ds(0, groups - 1)]
+        pltpu.make_async_copy(others, others, rs_send.at[h]).wait()
 
 
 def body(matrix, flip_bits, sample_rows):
@@ -313,19 +363,20 @@
         scratch_shapes=[
             pltpu.VMEM((rows // LANES, LANES), i32),
             pltpu.VMEM((samples // LANES, LANES), i32),
-            pltpu.VMEM((4, rows, width), f32),
+            pltpu.VMEM((rows, width), f32),
+            pltpu.VMEM((2, 4, rows // 2, width), f32),
             pltpu.VMEM((3, rows // LANES, LANES), i32),
             pltpu.VMEM((samples // 2, LANES), i32),
             pltpu.VMEM((groups * own, LANES), i32),
             pltpu.VMEM((groups * own, rows), jnp.bfloat16),
-            pltpu.VMEM((groups, own, width), f32),
-            pltpu.VMEM((groups, own, width), f32),
+            pltpu.VMEM((2, groups, own // 2, width), f32),
+            pltpu.VMEM((2, groups, own // 2, width), f32),
             pltpu.VMEM((chunks, chunk, width), f32),
             pltpu.VMEM((devices, chunk, width), f32),
             pltpu.VMEM((chunks, chunk, width), f32),
             pltpu.VMEM((chunk, width), f32),
-            dma((3,)), dma, dma, dma((pieces,)), dma((pieces,)), dma((pieces,)), dma((pieces,)),
-            dma((3,)), dma((3,)), dma, dma, dma, dma, dma, dma,
+            dma((3,)), dma((2,)), dma((2,)), dma((pieces,)), dma((pieces,)), dma((pieces,)), dma((pieces,)),
+            dma((3,)), dma((3,)), dma((2,)), dma((2,)), dma, dma, dma, dma,
             pltpu.SemaphoreType.REGULAR((16,)),
         ],
         compiler_params=pltpu.CompilerParams(collective_id=0, has_side_effects=True),

time: 33.4 us -> 33.2 us (level)
  no operation moved by 1% of the time
where the time goes in v3:
time: 33.2 us; the launch traced here: 33 us
  Pallas kernels  31.1 us (94%)
  local copies, waits for them, and re-layouts  1.25 us (4%)
  between operations  0.64 us (2%)
    pallas_call x1, Pallas kernels, body(): pl.pallas_call(functools.partial(kernel, n_grp, n_dev, rows, own), out_sh...  31.1 us
    unnamed x2, local copies, waits for them, and re-layouts  1.25 us

profile of v3, /device:TPU:0, one launch (start us, length us, event | category | flops | bytes accessed | tf_op | source)
XLA Modules:
  0.0 33.0 jit_solution(2590811792750855041)
XLA Ops:
  0.6 31.1 %shard_map.50 = (f32[64,128]{1,0:T(8,128)S(1)}, f32[128,128]{1,0:T(8,128)S(1)}) custom-call(f32[512,128]{1,0:T(8,128)} %x_ref.1, s32[4,128]{1,0:T(4,128)} %bitcast.3, s32[16,128]{1,0:T(8,128)} %bitcast.2), custom_call_target="tpu_custom_call" | custom-call | tf_op jit(solution)/shard_map/pallas_call | solution.py:355
  31.8 0.6 %copy.7 = f32[64,128]{1,0:T(8,128)} copy(f32[64,128]{1,0:T(8,128)S(1)} %get-tuple-element.2) | data formatting | bytes 65536
  32.4 0.6 %copy.8 = f32[128,128]{1,0:T(8,128)} copy(f32[128,128]{1,0:T(8,128)S(1)} %get-tuple-element.3) | data formatting | bytes 131072

commit v4 on v3

--- a/solution.py
+++ b/solution.py
@@ -192,6 +192,11 @@
         lane = lax.broadcasted_iota(jnp.int32, (picks, LANES), 1) + k * LANES
         base[:, k * LANES:(k + 1) * LANES] = sign_of(wanted & lane, row_bits).astype(jnp.bfloat16)
 
+    owner_signs = [
+        sign_of(wanted & ((grp * n_dev + dev) * rows), all_bits)
+        for grp, dev in ((me_g, me_d), (pair_g, me_d), (me_g, twin_d), (pair_g, twin_d))
+    ]
+
     def term(h, slot, flip_bits, grp, dev):
         signs = base[...]
         toggles = (1 - 2 * flip_bits).astype(f32).astype(jnp.bfloat16)
@@ -214,8 +219,7 @@
         )
         product = jnp.dot(signs, right, preferred_element_type=f32)
         first, last = product[:, :width], product[:, width:]
-        place = (grp * n_dev + dev) * rows
-        return (first + swap(first) + last) * sign_of(wanted & place, all_bits)
+        return (first + swap(first) + last) * owner_signs[slot]
 
     def give(h, i, j):
         to_y, to_z = lax.rem(y + i, n_y), lax.rem(z + j, n_z)

time: 33.2 us -> 33.2 us (level)
  no operation moved by 1% of the time
where the time goes in v4:
time: 33.2 us; the launch traced here: 33 us
  Pallas kernels  31.1 us (94%)
  local copies, waits for them, and re-layouts  1.25 us (4%)
  between operations  0.64 us (2%)
    pallas_call x1, Pallas kernels, body(): pl.pallas_call(functools.partial(kernel, n_grp, n_dev, rows, own), out_sh...  31.1 us
    unnamed x2, local copies, waits for them, and re-layouts  1.25 us

profile of v4, /device:TPU:0, one launch (start us, length us, event | category | flops | bytes accessed | tf_op | source)
XLA Modules:
  0.0 33.0 jit_solution(4671183634231502082)
XLA Ops:
  0.6 31.1 %shard_map.50 = (f32[64,128]{1,0:T(8,128)S(1)}, f32[128,128]{1,0:T(8,128)S(1)}) custom-call(f32[512,128]{1,0:T(8,128)} %x_ref.1, s32[4,128]{1,0:T(4,128)} %bitcast.3, s32[16,128]{1,0:T(8,128)} %bitcast.2), custom_call_target="tpu_custom_call" | custom-call | tf_op jit(solution)/shard_map/pallas_call | solution.py:359
  31.8 0.6 %copy.7 = f32[64,128]{1,0:T(8,128)} copy(f32[64,128]{1,0:T(8,128)S(1)} %get-tuple-element.2) | data formatting | bytes 65536
  32.4 0.6 %copy.8 = f32[128,128]{1,0:T(8,128)} copy(f32[128,128]{1,0:T(8,128)S(1)} %get-tuple-element.3) | data formatting | bytes 131072
